TPU v7x, 128 devices: a whole 4x4x4 slice. The times are simulated.
128 devices in a mesh: row: 4 (over y), col: 32 (over x, z, core).
Axes of the slice: x: 4, y: 4, z: 4, core: 2. Of those that a mesh axis runs over, the one named last changes fastest.
Arguments:
- charges: float32 [16, 32, 16, 256], P('row', 'col'), may hold values from -6 to 6
- column_order: int32 [32], replicated, may hold values from 0 to 31, as said below
- vertices: float32 [3, 66177], replicated, as said below
- panel_vertices: int32 [3, 131072], replicated, may hold values from 0 to 66176, as said below
- near_pairs: int32 [2, 2048], replicated, may hold values from 0 to 511, as said below
Outputs:
- potential_one: float32 [16, 32, 16, 256], P('row', 'col')
- potential_two: float32 [16, 32, 16, 256], P('row', 'col')
Inputs may be any that keep to these rules, and one draw needn't show every extreme that they name: column_order is a permutation of 0 to 31. `panel_vertices`: panels b * 256 to (b + 1) * 256 - 1 cover block b, a patch of 8 x 16 lattice quads each cut into two triangles along one of its diagonals; vertex ids are lattice row * 513 + lattice column. `vertices`: a jittered lattice of spacing 1.8 in x and y with heights in z; every panel has positive area. `near_pairs`: each column is a pair of distinct block ids, lower first, listed once; the higher block lies at most 3 grid rows below and within squared grid distance 12 of the lower one; entries 512 * b to 512 * (b + 1) - 1 are exactly the pairs whose lower block lies in grid rows 4 * b to 4 * (b + 1) - 1.
All inputs are finite; a program needn't handle non-finite values.
Results may differ from a plain program's by a relative error of at most 0.0003.
Values sent between devices are 32-bit elements; how exact they have to be, the bound alone decides.
A program may use at most 320 MiB of HBM per device.

v0:
```python
import math

import jax
import jax.numpy as jnp
import numpy as np
from jax import lax
from jax.sharding import PartitionSpec as P

PANELS = 256


group_size = 8


def shifted(value, axis, by):
    length = lax.axis_size(axis)
    pairs = [(i, i + by) for i in range(length) if 0 <= i + by < length]
    return lax.ppermute(value, axis, pairs)


def rule_tables():
    gauss_two = np.array([-1.0, 1.0]) / math.sqrt(3.0)
    gauss_four = np.array(
        [-0.8611363115940526, -0.3399810435848563, 0.3399810435848563, 0.8611363115940526]
    )
    weight_four = np.array(
        [0.3478548451374538, 0.6521451548625461, 0.6521451548625461, 0.3478548451374538]
    )
    corner_weights = []
    point_weights = []
    for first_index in range(2):
        for second_index in range(4):
            along = 0.5 * (1.0 + gauss_two[first_index])
            across = 0.5 * (1.0 + gauss_four[second_index])
            corner_weights.append([along, (1.0 - along) * across, (1.0 - along) * (1.0 - across)])
            point_weights.append(2.0 * 0.5 * 0.5 * weight_four[second_index] * (1.0 - along))
    return (np.array(corner_weights), np.array(point_weights))


def block_geometry(vertices, panel_vertices, block_ids):

    def take_block(block_id):
        return lax.dynamic_slice_in_dim(panel_vertices, block_id * PANELS, PANELS, 1)

    indices = jax.vmap(take_block)(block_ids)
    corners = jnp.moveaxis(vertices[:, indices], 0, 1)
    centre = (corners[:, :, 0] + corners[:, :, 1] + corners[:, :, 2]) / 3.0
    first_edge = corners[:, :, 1] - corners[:, :, 0]
    second_edge = corners[:, :, 2] - corners[:, :, 0]
    normal_x = first_edge[:, 1] * second_edge[:, 2] - first_edge[:, 2] * second_edge[:, 1]
    normal_y = first_edge[:, 2] * second_edge[:, 0] - first_edge[:, 0] * second_edge[:, 2]
    normal_z = first_edge[:, 0] * second_edge[:, 1] - first_edge[:, 1] * second_edge[:, 0]
    panel_area = 0.5 * jnp.sqrt(normal_x * normal_x + normal_y * normal_y + normal_z * normal_z)
    corner_weights, _ = rule_tables()
    points = jnp.einsum(
        "kc,gxcp->gxkp",
        jnp.asarray(corner_weights, corners.dtype),
        corners,
        precision=lax.Precision.HIGHEST,
    )
    return (centre, points, panel_area)


def tile_block(target, source):
    target_centre, target_points, target_area = target
    source_centre, source_points, source_area = source
    _, point_weights = rule_tables()
    kernel_sum = jnp.zeros(
        (target_centre.shape[0], target_centre.shape[2], source_centre.shape[2]), jnp.float32
    )
    for point_index in range(8):
        weight = float(point_weights[point_index])
        distance = target_centre[:, :, :, None] - source_points[:, :, point_index, None, :]
        kernel_sum = kernel_sum + weight / jnp.sqrt(jnp.sum(distance * distance, axis=1) + 0.01)
        distance = target_points[:, :, point_index, :, None] - source_centre[:, :, None, :]
        kernel_sum = kernel_sum + weight / jnp.sqrt(jnp.sum(distance * distance, axis=1) + 0.01)
    return kernel_sum * target_area[:, :, None] * source_area[:, None, :] / (8.0 * math.pi)


def apply_tiles(source_values, tile_stack):
    return jnp.einsum("grq,gpq->grp", source_values, tile_stack, precision=lax.Precision.HIGHEST)


def apply_transposed(source_values, tile_stack):
    return jnp.einsum("grp,gpq->grq", source_values, tile_stack, precision=lax.Precision.HIGHEST)


def look_up(lookup_table, lookup_index):
    matches = lookup_index[:, None] == jnp.arange(lookup_table.shape[0], dtype=jnp.int32)[None, :]
    return jnp.sum(jnp.where(matches, lookup_table[None, :], 0), axis=1)


def group_total(amount):
    return (amount + group_size - 1) // group_size


def fill_tiles(vertices, panel_vertices, target_ids, source_ids, amount):
    slot_total = target_ids.shape[0]
    buffer = jnp.zeros((slot_total, PANELS, PANELS), jnp.float32)

    def make_group(counter, carried):
        start = (counter * group_size).astype(jnp.int32)
        target_pick = lax.dynamic_slice_in_dim(target_ids, start, group_size, 0)
        source_pick = lax.dynamic_slice_in_dim(source_ids, start, group_size, 0)
        tile_stack = tile_block(
            block_geometry(vertices, panel_vertices, target_pick),
            block_geometry(vertices, panel_vertices, source_pick),
        )
        return lax.dynamic_update_slice_in_dim(carried, tile_stack, start, 0)

    return lax.fori_loop(0, group_total(amount), make_group, buffer)


def prepare(column_order, vertices, panel_vertices, near_pairs, band_rows):
    columns = lax.axis_size("col")
    band_count = lax.axis_size("row")
    band_index = lax.axis_index("row")
    column_index = lax.axis_index("col")
    positions = jnp.arange(columns, dtype=jnp.int32)
    position_of = jnp.sum(
        jnp.where(column_order[:, None] == positions[None, :], positions[:, None], 0), axis=0
    )
    home_column = jnp.sum(jnp.where(positions == column_index, column_order, 0))
    first_row = band_index * band_rows
    own_blocks = (first_row + jnp.arange(band_rows, dtype=jnp.int32)) * columns + home_column
    own_geometry = block_geometry(vertices, panel_vertices, own_blocks)
    self_tiles = tile_block(own_geometry, own_geometry)
    band_pairs = near_pairs.shape[1] // band_count
    segment = lax.dynamic_slice_in_dim(near_pairs, band_index * band_pairs, band_pairs, 1)
    low_blocks = segment[0]
    high_blocks = segment[1]
    chosen = look_up(position_of, low_blocks % columns) == column_index
    ranked = jnp.argsort(jnp.where(chosen, 0, 1).astype(jnp.int32), stable=True)
    first_slot = jnp.int32(0)
    amount = jnp.sum(chosen.astype(jnp.int32))
    slot_cap = min(band_pairs, 18 * band_rows)
    slot_total = group_total(slot_cap) * group_size
    slot_offsets = jnp.arange(slot_total, dtype=jnp.int32)
    picked = ranked[jnp.clip(slot_offsets, 0, band_pairs - 1)]
    low_pick = low_blocks[picked]
    high_pick = high_blocks[picked]
    live_weight = (slot_offsets < amount).astype(jnp.float32)
    low_row = low_pick // columns - first_row
    high_row = high_pick // columns - first_row
    low_pos = look_up(position_of, low_pick % columns)
    high_pos = look_up(position_of, high_pick % columns)
    tile_buffer = fill_tiles(vertices, panel_vertices, low_pick, high_pick, amount)
    slot_table = (low_row, low_pos, high_row, high_pos, live_weight)
    return (self_tiles, tile_buffer, slot_table, amount)


def near_product(block_values, prepared):
    self_tiles, tile_buffer, slot_table, amount = prepared
    band_rows = block_values.shape[0]
    columns = lax.axis_size("col")
    self_term = apply_tiles(block_values[:, 0], self_tiles)
    tail_shape = block_values.shape[2:]

    def slot_slice(values, start):
        return lax.dynamic_slice_in_dim(values, start, group_size, 0)

    later = shifted(block_values, "row", -1)
    own_band, later_band = (
        lax.all_gather(block_values, "col", axis=1, tiled=True),
        lax.all_gather(later, "col", axis=1, tiled=True),
    )
    source_table = jnp.concatenate([own_band, later_band], axis=0)

    def visit_pairs(counter, carried):
        start = (counter * group_size).astype(jnp.int32)
        tile_stack = slot_slice(tile_buffer, start)
        low_row, low_pos, high_row, high_pos, live_weight = [
            slot_slice(entry, start) for entry in slot_table
        ]
        weight = live_weight[:, None, None]
        to_low = apply_tiles(source_table[high_row, high_pos], tile_stack) * weight
        to_high = apply_transposed(source_table[low_row, low_pos], tile_stack) * weight
        return carried.at[low_row, low_pos].add(to_low).at[high_row, high_pos].add(to_high)

    partial_value = jnp.zeros((2 * band_rows, columns) + tail_shape, jnp.float32)
    partial_value = lax.fori_loop(0, group_total(amount), visit_pairs, partial_value)
    summed = lax.psum_scatter(partial_value, "col", scatter_dimension=1, tiled=True)
    carried_down = shifted(summed[band_rows:], "row", 1)
    return summed[:band_rows] + carried_down + self_term[:, None]


def body(charges, column_order, vertices, panel_vertices, near_pairs):
    prepared = prepare(column_order, vertices, panel_vertices, near_pairs, charges.shape[0])
    potential_one = near_product(charges, prepared)
    potential_two = near_product(potential_one, prepared)
    return (potential_one, potential_two)


def solution(mesh):
    return jax.shard_map(
        body,
        mesh=mesh,
        in_specs=(P("row", "col", None, None), P(), P(), P(), P()),
        out_specs=(P("row", "col", None, None), P("row", "col", None, None)),
        check_vma=False,
    )
```

profile of v0, /device:TPU:8, one launch (start us, length us, event | category | flops | bytes accessed | tf_op | source)
XLA Modules:
  0.0 1595.9 jit_solution(12323723513290583118)
XLA Ops:
  13.7 16.3 %copy.209 = f32[3,66177]{0,1:T(8,128)} copy(f32[3,66177]{1,0:T(4,128)} %param.16) | data formatting | bytes 1588248
  30.0 3.8 sort.17
  39.4 8.8 broadcast_in_dim.83
  48.2 145.2 %while.48 = (s32[]{:T(128)}, f32[72,256,256]{2,1,0:T(8,128)}, s32[]{:T(128)}, s32[72]{0:T(128)}, s32[3,131072]{1,0:T(4,128)}, /*index=5*/f32[3,66177]{0,1:T(8,12...) while((s32[]{:T(128)}, f32[72,256,256]{2,1,0:T(8,128)}, ...), condition=%wide.region_21.22_spmd.clone.clone, body=%wide.region_4.21_spmd.sunk.clone.clone.sunk | while | flops 96510024 | bytes 99630584 | solution.py:111
  49.0 17.1 %while.49 = (s32[]{:T(128)}, s32[3,131072]{1,0:T(4,128)}, s32[8,2]{0,1:T(2,128)S(1)}, s32[8,3,256]{2,1,0:T(4,128)S(1)}, s32[]{:T(128)}) while((s32[]{:T(128)}, s32[3,131072]{1,0:T(4,128)}, s32[8,2]{0,1:T(2,128)S(1)}, s32[8,3,256]{2,1,0:T(4,128)S(1)}, s32[]{:T(128)}) %tuple.208), condition=%wide.while_cond.1, body=%wide.while_body.1.sunk | while | flops 2 | bytes 7265 | solution.py:43
  66.1 26.8 %gather_fusion.4 = f32[6144,3]{1,0:T(8,128)S(1)} fusion(f32[3,66177]{0,1:T(8,128)} %get-tuple-element.922, s32[6144]{0:T(1024)S(1)} %broadcast_clamp_fusion.5), kind=kCustom, calls=%fused_computation.5.clone.clone.1 | custom fusion | bytes 172032 | tf_op jit(solution)/shard_map/while/body/gather | solution.py:46
  95.3 17.1 %while.50 = (s32[]{:T(128)}, s32[3,131072]{1,0:T(4,128)}, s32[8,2]{0,1:T(2,128)S(1)}, s32[8,3,256]{2,1,0:T(4,128)S(1)}, s32[]{:T(128)}) while((s32[]{:T(128)}, s32[3,131072]{1,0:T(4,128)}, s32[8,2]{0,1:T(2,128)S(1)}, s32[8,3,256]{2,1,0:T(4,128)S(1)}, s32[]{:T(128)}) %tuple.211), condition=%wide.while_cond, body=%wide.while_body.sunk | while | flops 2 | bytes 7265 | solution.py:43
  112.4 31.7 %gather_fusion.5 = f32[6144,3]{1,0:T(8,128)} fusion(f32[3,66177]{0,1:T(8,128)} %get-tuple-element.922, s32[6144]{0:T(1024)S(1)} %broadcast_clamp_fusion.6), kind=kCustom, calls=%fused_computation.4.clone.clone.1 | custom fusion | bytes 172032 | tf_op jit(solution)/shard_map/while/body/gather | solution.py:46
  146.5 14.4 multiply_reduce_fusion.35
  166.2 14.5 multiply_reduce_fusion.34
  180.7 12.6 multiply_dynamic-update-slice_fusion.2
  195.5 4.6 pad_maximum_fusion
  202.7 16.1 %while.43 = (s32[]{:T(128)}, f32[8,32,16,256]{3,2,1,0:T(8,128)}, s32[]{:T(128)}, s32[72]{0:T(128)S(1)}, s32[72]{0:T(128)S(1)}, /*index=5*/s32[72]{0:T(128)S(1)},...) while((s32[]{:T(128)}, f32[8,32,16,256]{3,2,1,0:T(8,128)}, ...), condition=%wide.region_27.28_spmd, body=%wide.region_24.27_spmd.sunk | while | flops 201457920 | bytes 6030147 | solution.py:181
  202.8 2.8 gather_fusion
  205.6 3.4 fusion.138
  218.8 4.8 copy.210
  225.6 8.1 while.45
  233.7 18.8 %gather_fusion.9 = f32[3072,3]{1,0:T(8,128)S(1)} fusion(f32[3,66177]{0,1:T(8,128)} %get-tuple-element.1057, s32[3072]{0:T(1024)S(1)} %broadcast_clamp_fusion.2), kind=kCustom, calls=%fused_computation.9 | custom fusion | bytes 86016 | tf_op jit(solution)/shard_map/gather | solution.py:46
  254.1 13.2 multiply_reduce_fusion.31
  267.3 1004.5 %reduce-scatter.3.cloned.1.call-done = f32[8,1,16,256]{3,2,0,1:T(8,128)} async-done(((f32[8,32,16,256]{3,2,0,1:T(8,128)}), f32[8,1,16,256]{3,2,0,1:T(8,128)}) %reduce-scatter.3.cloned.1.call-update) | async-done | bytes 131088 | tf_op jit(solution)/shard_map/reduce_scatter | solution.py:182
  1272.7 3.3 collective-permute-start.1
  1276.1 6.4 fusion.78
  1286.8 3.9 collective-permute-done.2
  1291.3 36.0 %all-gather.9.cloned.1.call-done = f32[4,32,16,256]{3,2,0,1:T(8,128)} async-done(((f32[4,1,16,256]{3,2,0,1:T(8,128)}), f32[4,32,16,256]{3,2,0,1:T(8,128)}) %all-gather.9.cloned.1.call-update) | async-done | bytes 2097168 | tf_op jit(solution)/shard_map/all_gather | solution.py:164
  1327.3 46.2 %all-gather.11.cloned.1.call-done = f32[4,32,16,256]{3,2,0,1:T(8,128)} async-done(((f32[4,1,16,256]{3,2,0,1:T(8,128)}), f32[4,32,16,256]{3,2,0,1:T(8,128)}) %all-gather.11.cloned.1.call-update) | async-done | bytes 2097168 | tf_op jit(solution)/shard_map/all_gather | solution.py:165
  1381.1 16.1 %while.44 = (s32[]{:T(128)}, f32[8,32,16,256]{3,2,1,0:T(8,128)}, s32[]{:T(128)}, s32[72]{0:T(128)S(1)}, s32[72]{0:T(128)S(1)}, /*index=5*/s32[72]{0:T(128)S(1)},...) while((s32[]{:T(128)}, f32[8,32,16,256]{3,2,1,0:T(8,128)}, ...), condition=%wide.region_49.50_spmd, body=%wide.region_46.49_spmd.sunk | while | flops 201457920 | bytes 6030147 | solution.py:181
  1381.2 2.8 gather_fusion.2
  1384.0 3.4 fusion.145
  1397.2 4.8 copy.241
  1402.0 177.7 %reduce-scatter.5.cloned.1.call-done = f32[8,1,16,256]{3,2,0,1:T(8,128)} async-done(((f32[8,32,16,256]{3,2,0,1:T(8,128)}), f32[8,1,16,256]{3,2,0,1:T(8,128)}) %reduce-scatter.5.cloned.1.call-update) | async-done | bytes 131088 | tf_op jit(solution)/shard_map/reduce_scatter | solution.py:182
  1580.5 3.4 collective-permute-start.3
  1583.9 2.8 collective-permute-done.3
  (218 shorter events, 108.8 us)
Async XLA Ops:
  7.2 188.3 %all-gather.5.cloned.1.call-start = ((), (), s32[]{:S(2)}) async-start(), calls=%async_computation.2 | async-start | bytes 2162688 | tf_op jit(solution)/shard_map/all_gather | solution.py:164
  7.9 187.6 %all-gather.7.cloned.1.call-start = ((), (), s32[]{:S(2)}) async-start(), calls=%async_computation.3 | async-start | bytes 2162688 | tf_op jit(solution)/shard_map/all_gather | solution.py:165
  7.9 30.7 %collective-permute-start = (f32[4,1,16,256]{3,2,1,0:T(8,128)}, f32[4,1,16,256]{3,2,1,0:T(8,128)S(1)}, u32[]{:S(2)}, u32[]{:S(2)}) collective-permute-start(f32[4,1,16,256]{3,2,1,0:T(8,128)} %param.14), channel_id=1, source_target_pairs={{32,0},{64,32},{96,64},{33,1},{65,33},{97,65},{34,2},{66,34},{98,6... | collective-permute-start | bytes 196616 | tf_op jit(solution)/shard_map/ppermute | solution.py:18
  11.8 0.5 copy-start.11
  38.7 0.6 copy-start.9
  39.3 8.9 copy-start.6
  39.3 1232.5 %reduce-scatter.3.cloned.1.call-start = ((), (), s32[]{:S(2)}) async-start(), calls=%async_computation.4 | async-start | bytes 4325376 | tf_op jit(solution)/shard_map/reduce_scatter | solution.py:182
  166.1 14.5 copy-start.3
  166.1 14.6 copy-start
  166.2 14.6 copy-start.1
  166.2 14.6 copy-start.2
  180.7 12.6 copy-start.7
  223.6 0.7 copy-start.12
  223.7 1103.6 %all-gather.9.cloned.1.call-start = ((), (), s32[]{:S(2)}) async-start(), calls=%async_computation.5 | async-start | bytes 2162688 | tf_op jit(solution)/shard_map/all_gather | solution.py:164
  1272.7 9.8 collective-permute-start.1
  1276.1 6.5 copy-start.5
  1276.1 6.5 copy-start.8
  1284.2 89.3 %all-gather.11.cloned.1.call-start = ((), (), s32[]{:S(2)}) async-start(), calls=%async_computation.6 | async-start | bytes 2162688 | tf_op jit(solution)/shard_map/all_gather | solution.py:165
  1284.3 6.4 collective-permute-start.2
  1290.6 0.6 copy-start.10
  1291.3 288.3 %reduce-scatter.5.cloned.1.call-start = ((), (), s32[]{:S(2)}) async-start(), calls=%async_computation.7 | async-start | bytes 4325376 | tf_op jit(solution)/shard_map/reduce_scatter | solution.py:182
  1401.9 184.7 %copy-start.4 = (f32[4,1,16,256]{3,2,0,1:T(8,128)S(1)}, f32[4,1,16,256]{3,2,0,1:T(8,128)}, u32[]{:S(2)}) copy-start(f32[4,1,16,256]{3,2,0,1:T(8,128)} %fusion.81) | copy-start | bytes 196612
  1580.5 6.1 collective-permute-start.3
Sparse Core Ops, SparseCore 0:
  10.4 47.9 all-gather.4
  61.2 43.2 all-gather.6
  223.8 1048.0 reduce-scatter.2
  1284.3 42.9 all-gather.8
  1330.2 43.2 all-gather.10
  1402.1 177.4 reduce-scatter.4
where the time goes:
time: 1610 us; the launch traced here: 1600 us
  waiting for transfers between devices  1270 us (79%)
  local copies, waits for them, and re-layouts  192 us (12%)
  other arithmetic  87.5 us (5%)
  matrix products  17.3 us (1%)
    reduce_scatter x2, waiting for transfers between devices, near_product(): lax.psum_scatter(partial_value, 'col', scatter_dimension=1, tiled=True)  1180 us
    gather x6, local copies, waits for them, and re-layouts, block_geometry(): corners = jnp.moveaxis(vertices[:, indices], 0, 1)  81.3 us
    all_gather x2, waiting for transfers between devices, near_product(): lax.all_gather(later, 'col', axis=1, tiled=True)  46.2 us
    gather x60, local copies, waits for them, and re-layouts  42.2 us
    reduce_sum x3, other arithmetic, tile_block(): jnp.sum(distance * distance, axis=1) + 0.01  42.1 us
    all_gather x2, waiting for transfers between devices, near_product(): lax.all_gather(block_values, 'col', axis=1, tiled=True)  36 us
  transfers between devices with their start and end apart: 10, of which 6 were waited for; matrix products, arithmetic and copies ran while one was open for 15% of the time, Pallas kernels for 0%

commit v1 on v0

v1 whole, which is shorter than its diff:
```python
import math

import jax
import jax.numpy as jnp
import numpy as np
from jax import lax
from jax.sharding import PartitionSpec as P

PANELS = 256
REACH = 4


def shifted(value, axis, by):
    length = lax.axis_size(axis)
    pairs = [(i, i + by) for i in range(length) if 0 <= i + by < length]
    return lax.ppermute(value, axis, pairs)


def rule_tables():
    gauss_two = np.array([-1.0, 1.0]) / math.sqrt(3.0)
    gauss_four = np.array(
        [-0.8611363115940526, -0.3399810435848563, 0.3399810435848563, 0.8611363115940526]
    )
    weight_four = np.array(
        [0.3478548451374538, 0.6521451548625461, 0.6521451548625461, 0.3478548451374538]
    )
    corner_weights = []
    point_weights = []
    for first_index in range(2):
        for second_index in range(4):
            along = 0.5 * (1.0 + gauss_two[first_index])
            across = 0.5 * (1.0 + gauss_four[second_index])
            corner_weights.append([along, (1.0 - along) * across, (1.0 - along) * (1.0 - across)])
            point_weights.append(2.0 * 0.5 * 0.5 * weight_four[second_index] * (1.0 - along))
    return (np.array(corner_weights), np.array(point_weights))


def block_geometry(vertices, panel_vertices, block_ids):
    panels = panel_vertices.reshape(3, -1, PANELS)[:, block_ids]
    corners = jnp.transpose(vertices[:, panels], (2, 1, 0, 3))
    centre = (corners[:, 0] + corners[:, 1] + corners[:, 2]) / 3.0
    first_edge = corners[:, 1] - corners[:, 0]
    second_edge = corners[:, 2] - corners[:, 0]
    normal_x = first_edge[:, 1] * second_edge[:, 2] - first_edge[:, 2] * second_edge[:, 1]
    normal_y = first_edge[:, 2] * second_edge[:, 0] - first_edge[:, 0] * second_edge[:, 2]
    normal_z = first_edge[:, 0] * second_edge[:, 1] - first_edge[:, 1] * second_edge[:, 0]
    panel_area = 0.5 * jnp.sqrt(normal_x * normal_x + normal_y * normal_y + normal_z * normal_z)
    corner_weights, _ = rule_tables()
    points = jnp.einsum(
        "kc,gcxp->gxkp",
        jnp.asarray(corner_weights, corners.dtype),
        corners,
        precision=lax.Precision.HIGHEST,
    )
    return (centre, points, panel_area)


def tile_block(target, source):
    target_centre, target_points, target_area = target
    source_centre, source_points, source_area = source
    _, point_weights = rule_tables()
    kernel_sum = jnp.zeros(
        (target_centre.shape[0], target_centre.shape[2], source_centre.shape[2]), jnp.float32
    )
    for point_index in range(8):
        weight = float(point_weights[point_index])
        distance = target_centre[:, :, :, None] - source_points[:, :, point_index, None, :]
        kernel_sum = kernel_sum + weight * lax.rsqrt(jnp.sum(distance * distance, axis=1) + 0.01)
        distance = target_points[:, :, point_index, :, None] - source_centre[:, :, None, :]
        kernel_sum = kernel_sum + weight * lax.rsqrt(jnp.sum(distance * distance, axis=1) + 0.01)
    return kernel_sum * target_area[:, :, None] * source_area[:, None, :] / (8.0 * math.pi)


def apply_tiles(source_values, tile_stack):
    return jnp.einsum("grq,gpq->grp", source_values, tile_stack, precision=lax.Precision.HIGHEST)


def apply_transposed(source_values, tile_stack):
    return jnp.einsum("grp,gpq->grq", source_values, tile_stack, precision=lax.Precision.HIGHEST)


def prepare(column_order, vertices, panel_vertices, near_pairs, band_rows):
    columns = lax.axis_size("col")
    band_count = lax.axis_size("row")
    band_index = lax.axis_index("row")
    column_index = lax.axis_index("col")
    positions = jnp.arange(columns, dtype=jnp.int32)
    position_of = jnp.sum(
        jnp.where(column_order[:, None] == positions[None, :], positions[:, None], 0), axis=0
    )
    home_column = jnp.sum(jnp.where(positions == column_index, column_order, 0))
    first_row = band_index * band_rows
    own_blocks = (first_row + jnp.arange(band_rows, dtype=jnp.int32)) * columns + home_column
    band_pairs = near_pairs.shape[1] // band_count
    share = band_pairs // columns
    segment = lax.dynamic_slice_in_dim(
        near_pairs, band_index * band_pairs + column_index * share, share, 1
    )
    low_blocks = segment[0]
    high_blocks = segment[1]
    targets = jnp.concatenate([own_blocks, low_blocks])
    sources = jnp.concatenate([own_blocks, high_blocks])
    tiles = tile_block(
        block_geometry(vertices, panel_vertices, targets),
        block_geometry(vertices, panel_vertices, sources),
    )
    self_tiles = tiles[:band_rows]
    pair_tiles = tiles[band_rows:]
    low_row = low_blocks // columns - first_row
    high_row = high_blocks // columns - first_row
    low_pos = position_of[low_blocks % columns]
    high_pos = position_of[high_blocks % columns]
    slot_table = (low_row, low_pos, high_row, high_pos)
    return (self_tiles, pair_tiles, slot_table)


def near_product(block_values, prepared):
    self_tiles, pair_tiles, slot_table = prepared
    band_rows = block_values.shape[0]
    low_row, low_pos, high_row, high_pos = slot_table
    self_term = apply_tiles(block_values[:, 0], self_tiles)
    later = shifted(block_values[:REACH], "row", -1)
    source_table = lax.all_gather(
        jnp.concatenate([block_values, later], axis=0), "col", axis=1, tiled=True
    )
    to_low = apply_tiles(source_table[high_row, high_pos], pair_tiles)
    to_high = apply_transposed(source_table[low_row, low_pos], pair_tiles)
    partial_value = jnp.zeros(source_table.shape, jnp.float32)
    partial_value = partial_value.at[low_row, low_pos].add(to_low).at[high_row, high_pos].add(to_high)
    summed = lax.psum_scatter(partial_value, "col", scatter_dimension=1, tiled=True)
    carried_down = shifted(summed[band_rows:], "row", 1)
    head = summed[:REACH] + carried_down
    own = jnp.concatenate([head, summed[REACH:band_rows]], axis=0)
    return own + self_term[:, None]


def body(charges, column_order, vertices, panel_vertices, near_pairs):
    prepared = prepare(column_order, vertices, panel_vertices, near_pairs, charges.shape[0])
    potential_one = near_product(charges, prepared)
    potential_two = near_product(potential_one, prepared)
    return (potential_one, potential_two)


def solution(mesh):
    return jax.shard_map(
        body,
        mesh=mesh,
        in_specs=(P("row", "col", None, None), P(), P(), P(), P()),
        out_specs=(P("row", "col", None, None), P("row", "col", None, None)),
        check_vma=False,
    )
```

time: 1610 us -> 582 us (0.36)
  waiting for transfers between devices: 1270 us -> 222 us
  other arithmetic: 87.5 us -> 112 us
    reduce_scatter x2, waiting for transfers between devices: 1180 us -> 166 us  [near_product(): lax.psum_scatter(partial_value, 'col', scatter_dimension=1, tiled=True)]
    all_gather x4 -> x2, waiting for transfers between devices: 82.2 us -> 45.5 us  [near_product(): lax.all_gather(jnp.concatenate([block_values, later], axis=0), 'col', axi...]
    reduce_sum x3 -> x2, other arithmetic: 42.1 us -> 68 us  [tile_block(): jnp.sum(distance * distance, axis=1) + 0.01]
    div x1, other arithmetic: 6.44 us -> 29.1 us  [tile_block(): kernel_sum * target_area[:, :, None] * source_area[:, None, :]]
    gather x73 -> x12, local copies, waits for them, and re-layouts: 139 us -> 148 us  [the longest x4 135 us: block_geometry(): corners = jnp.transpose(vertices[:, panels], (2, 1, 0, 3))]
  transfers between devices with their start and end apart: 10 -> 8, of which waited for: 6 -> 6; matrix products, arithmetic and copies ran while one was open for 15% -> 46% of each run, Pallas kernels for 0% -> 0%
where the time goes in v1:
time: 582 us; the launch traced here: 581 us
  waiting for transfers between devices  222 us (38%)
  local copies, waits for them, and re-layouts  195 us (34%)
  other arithmetic  112 us (19%)
  matrix products  26.2 us (5%)
  between operations  14.4 us (2%)
  starting transfers between devices  11.7 us (2%)
    reduce_scatter x2, waiting for transfers between devices, near_product(): lax.psum_scatter(partial_value, 'col', scatter_dimension=1, tiled=True)  166 us
    gather x4, local copies, waits for them, and re-layouts, block_geometry(): corners = jnp.transpose(vertices[:, panels], (2, 1, 0, 3))  135 us
    reduce_sum x2, other arithmetic, tile_block(): jnp.sum(distance * distance, axis=1) + 0.01  68 us
    all_gather x2, waiting for transfers between devices, near_product(): lax.all_gather(jnp.concatenate([block_values, later], axis=0), 'col', axi...  45.5 us
    div x1, other arithmetic, tile_block(): kernel_sum * target_area[:, :, None] * source_area[:, None, :]  29.1 us
    dot_general x4, matrix products, apply_tiles(): jnp.einsum('grq,gpq->grp', source_values, tile_stack, precision=lax.Preci...  16.4 us
    unnamed x13, local copies, waits for them, and re-layouts  16.3 us
  transfers between devices with their start and end apart: 8, of which 6 were waited for; matrix products, arithmetic and copies ran while one was open for 46% of the time, Pallas kernels for 0%

profile of v1, /device:TPU:8, one launch (start us, length us, event | category | flops | bytes accessed | tf_op | source)
XLA Modules:
  0.0 580.7 jit_solution(6145317578535073538)
XLA Ops:
  13.9 16.3 %copy.111 = f32[3,66177]{0,1:T(8,128)} copy(f32[3,66177]{1,0:T(4,128)} %param.9) | data formatting | bytes 1588248 | tf_op args[2]
  30.2 62.1 %gather_fusion.6 = f32[15360,3]{1,0:T(8,128)} fusion(f32[3,66177]{0,1:T(8,128)} %copy.111, s32[15360]{0:T(1024)S(1)} %broadcast_clamp_fusion), kind=kCustom, calls=%fused_computation.6 | custom fusion | bytes 430080 | tf_op jit(solution)/shard_map/gather | solution.py:40
  92.3 5.7 copy.117
  99.6 62.1 %gather_fusion.4 = f32[15360,3]{1,0:T(8,128)} fusion(f32[3,66177]{0,1:T(8,128)} %copy.111, s32[15360]{0:T(1024)S(1)} %broadcast_clamp_fusion.1), kind=kCustom, calls=%fused_computation.4 | custom fusion | bytes 430080 | tf_op jit(solution)/shard_map/gather | solution.py:40
  161.7 5.3 copy.112
  167.1 5.7 copy.120
  173.7 5.3 copy.116
  182.5 34.1 %multiply_reduce_fusion.15 = (f32[20,256,256]{2,1,0:T(8,128)}, f32[20,256,256]{2,1,0:T(8,128)}, f32[20,256,256]{2,1,0:T(8,128)}, f32[20,256,256]{2,1,0:T(8,128)}...) fusion(f32[20,3,256]{2,1,0:T(4,128)S(1)} %copy.119, ...), kind=kLoop, calls=%fused_computation.29 | loop fusion | flops 83886080 | bytes 42496000 | tf_op jit(solution)/shard_map/reduce_sum | solution.py:68
  216.5 33.9 %multiply_reduce_fusion.14 = (f32[20,256,256]{2,1,0:T(8,128)}, f32[20,256,256]{2,1,0:T(8,128)}, f32[20,256,256]{2,1,0:T(8,128)}, f32[20,256,256]{2,1,0:T(8,128)}...) fusion(f32[20,3,256]{2,1,0:T(4,128)S(1)} %copy.123, ...), kind=kLoop, calls=%fused_computation.28 | loop fusion | flops 83886080 | bytes 42496000 | tf_op jit(solution)/shard_map/reduce_sum | solution.py:70
  250.5 29.1 %fusion.15 = f32[20,256,256]{2,1,0:T(8,128)} fusion(f32[20,256,256]{2,1,0:T(8,128)} %get-tuple-element.25, f32[20,256,256]{2,1,0:T(8,128)} %get-tuple-element.17, f32[20,256,256]{2,1,0:T(8,128)} %get-tuple-element.24, f32[20,256,256]{2,1,0:T(8,128)} %get-tuple-element.16, f32[20,256,256]{2,1,0:T(8,128)} %get-tuple-element.23, ...), kind=kLoop, calls=%fused_computation.46 | loop fusion | flops 64225280 | bytes 89169920 | tf_op jit(solution)/shard_map/div | solution.py:71
  279.6 2.8 gather_fusion.2
  282.4 5.7 fusion.22
  288.0 2.8 gather_fusion.7
  290.8 4.3 fusion.20
  297.7 2.6 scatter_fusion
  302.9 4.8 copy.152
  307.9 84.7 %reduce-scatter.3.cloned.1.call-done = f32[8,1,16,256]{3,2,0,1:T(8,128)} async-done(((f32[8,32,16,256]{3,2,0,1:T(8,128)}), f32[8,1,16,256]{3,2,0,1:T(8,128)}) %reduce-scatter.3.cloned.1.call-update) | async-done | bytes 131088 | tf_op jit(solution)/shard_map/reduce_scatter | solution.py:130
  393.4 3.4 collective-permute-start.1
  396.8 2.8 collective-permute-done.1
  403.7 4.2 collective-permute-done.2
  408.9 45.5 %all-gather.5.cloned.1.call-done = f32[8,32,16,256]{3,2,0,1:T(8,128)} async-done(((f32[8,1,16,256]{3,2,0,1:T(8,128)}), f32[8,32,16,256]{3,2,0,1:T(8,128)}) %all-gather.5.cloned.1.call-update) | async-done | bytes 4194320 | tf_op jit(solution)/shard_map/all_gather | solution.py:123
  454.4 2.8 gather_fusion.9
  457.2 4.3 fusion.16
  461.5 2.8 gather_fusion.8
  464.3 5.7 fusion.18
  469.9 2.6 broadcast.447
  472.6 2.6 scatter_fusion.2
  477.8 4.8 copy.153
  482.7 81.7 %reduce-scatter.5.cloned.1.call-done = f32[8,1,16,256]{3,2,0,1:T(8,128)} async-done(((f32[8,32,16,256]{3,2,0,1:T(8,128)}), f32[8,1,16,256]{3,2,0,1:T(8,128)}) %reduce-scatter.5.cloned.1.call-update) | async-done | bytes 131088 | tf_op jit(solution)/shard_map/reduce_scatter | solution.py:130
  565.2 3.4 collective-permute-start.3
  568.6 2.7 collective-permute-done.3
  571.3 2.8 fusion.30
  (100 shorter events, 27.0 us)
Async XLA Ops:
  7.2 6.0 %copy-start = (s32[3,131072]{1,0:T(4,128)S(1)}, s32[3,131072]{1,0:T(4,128)}, u32[]{:S(2)}) copy-start(s32[3,131072]{1,0:T(4,128)} %param.10) | copy-start | bytes 4718596
  7.2 272.4 %all-gather.3.cloned.1.call-start = ((), (), s32[]{:S(2)}) async-start(), calls=%async_computation.2 | async-start | bytes 4325376 | tf_op jit(solution)/shard_map/all_gather | solution.py:123
  7.2 174.3 %collective-permute-start = (f32[4,1,16,256]{3,2,1,0:T(8,128)}, f32[4,1,16,256]{3,2,1,0:T(8,128)S(1)}, u32[]{:S(2)}, u32[]{:S(2)}) collective-permute-start(f32[4,1,16,256]{3,2,1,0:T(8,128)} %param.7), channel_id=1, source_target_pairs={{32,0},{64,32},{96,64},{33,1},{65,33},{97,65},{34,2},{66,34},{98,6... | collective-permute-start | bytes 196616 | tf_op jit(solution)/shard_map/ppermute | solution.py:16
  30.2 67.7 %copy-start.5 = (f32[8,3,1,1]{0,1,3,2:T(4,128)S(1)}, f32[8,3,1,1]{0,1,3,2:T(4,128)}, u32[]{:S(2)}) copy-start(f32[8,3,1,1]{0,1,3,2:T(4,128)} %constant.210) | copy-start | bytes 292
  179.0 2.6 copy-start.4
  182.2 210.3 %reduce-scatter.3.cloned.1.call-start = ((), (), s32[]{:S(2)}) async-start(), calls=%async_computation.3 | async-start | bytes 4325376 | tf_op jit(solution)/shard_map/reduce_scatter | solution.py:130
  216.5 33.9 %copy-start.2 = (f32[20,256,256]{2,1,0:T(8,128)S(1)}, f32[20,256,256]{2,1,0:T(8,128)}, u32[]{:S(2)}) copy-start(f32[20,256,256]{2,1,0:T(8,128)} %get-tuple-element.10) | copy-start | bytes 15728644
  307.8 146.6 %all-gather.5.cloned.1.call-start = ((), (), s32[]{:S(2)}) async-start(), calls=%async_computation.4 | async-start | bytes 4325376 | tf_op jit(solution)/shard_map/all_gather | solution.py:123
  393.4 6.1 %collective-permute-start.1 = (f32[4,1,16,256]{3,2,0,1:T(8,128)S(1)}, f32[4,1,16,256]{3,2,0,1:T(8,128)S(1)}, u32[]{:S(2)}, u32[]{:S(2)}) collective-permute-start(f32[4,1,16,256]{3,2,0,1:T(8,128)S(1)} %slice.252), channel_id=1, source_target_pairs={{0,32},{32,64},{64,96},{1,33},{33,65},{65,97},{2,34},{34,66},{66,9... | collective-permute-start | bytes 196616 | tf_op jit(solution)/shard_map/ppermute | solution.py:16
  401.8 169.6 %copy-start.3 = (f32[4,1,16,256]{3,2,0,1:T(8,128)}, f32[4,1,16,256]{3,2,0,1:T(8,128)S(1)}, u32[]{:S(2)}) copy-start(f32[4,1,16,256]{3,2,0,1:T(8,128)S(1)} %fusion.31) | copy-start | bytes 196612
  401.8 6.2 %collective-permute-start.2 = (f32[4,1,16,256]{3,2,0,1:T(8,128)S(1)}, f32[4,1,16,256]{3,2,0,1:T(8,128)S(1)}, u32[]{:S(2)}, u32[]{:S(2)}) collective-permute-start(f32[4,1,16,256]{3,2,0,1:T(8,128)S(1)} %fusion.31), channel_id=1, source_target_pairs={{32,0},{64,32},{96,64},{33,1},{65,33},{97,65},{34,2},{66,34},{98,6... | collective-permute-start | bytes 196616 | tf_op jit(solution)/shard_map/ppermute | solution.py:16
  408.6 155.7 %reduce-scatter.5.cloned.1.call-start = ((), (), s32[]{:S(2)}) async-start(), calls=%async_computation.5 | async-start | bytes 4325376 | tf_op jit(solution)/shard_map/reduce_scatter | solution.py:130
  475.2 98.9 %copy-start.1 = (s32[3,131072]{1,0:T(4,128)S(1)}, s32[3,131072]{1,0:T(4,128)}, u32[]{:S(2)}) copy-start(s32[3,131072]{1,0:T(4,128)} %param.10) | copy-start | bytes 4718596
  565.2 6.1 %collective-permute-start.3 = (f32[4,1,16,256]{3,2,0,1:T(8,128)S(1)}, f32[4,1,16,256]{3,2,0,1:T(8,128)S(1)}, u32[]{:S(2)}, u32[]{:S(2)}) collective-permute-start(f32[4,1,16,256]{3,2,0,1:T(8,128)S(1)} %slice.254), channel_id=1, source_target_pairs={{0,32},{32,64},{64,96},{1,33},{33,65},{65,97},{2,34},{34,66},{66,9... | collective-permute-start | bytes 196616 | tf_op jit(solution)/shard_map/ppermute | solution.py:16
Sparse Core Ops, SparseCore 0:
  182.3 48.8 all-gather.2
  307.9 84.5 reduce-scatter.2
  408.7 45.6 all-gather.4
  482.8 81.4 reduce-scatter.4

commit v2 on v1

--- a/solution.py
+++ b/solution.py
@@ -8,6 +8,8 @@
 
 PANELS = 256
 REACH = 4
+QUAD_ROWS = 8
+QUAD_COLS = 16
 
 
 def shifted(value, axis, by):
@@ -35,9 +37,32 @@
     return (np.array(corner_weights), np.array(point_weights))
 
 
-def block_geometry(vertices, panel_vertices, block_ids):
+def block_corners(vertices, panel_vertices, block_ids, lattice_cols):
+    patch_rows, patch_cols = QUAD_ROWS + 1, QUAD_COLS + 1
     panels = panel_vertices.reshape(3, -1, PANELS)[:, block_ids]
-    corners = jnp.transpose(vertices[:, panels], (2, 1, 0, 3))
+    lattice_row = panels // lattice_cols
+    lattice_col = panels % lattice_cols
+    base_row = jnp.min(lattice_row, axis=(0, 2))
+    base_col = jnp.min(lattice_col, axis=(0, 2))
+    local = (lattice_row - base_row[None, :, None]) * patch_cols + (
+        lattice_col - base_col[None, :, None]
+    )
+    grid = vertices.reshape(3, -1, lattice_cols)
+
+    def take_patch(row, col):
+        return lax.dynamic_slice(grid, (0, row, col), (3, patch_rows, patch_cols))
+
+    patch = jax.vmap(take_patch)(base_row, base_col).reshape(
+        block_ids.shape[0], 3, patch_rows * patch_cols
+    )
+    pick = (
+        local[:, :, :, None] == jnp.arange(patch_rows * patch_cols, dtype=jnp.int32)
+    ).astype(jnp.float32)
+    return jnp.einsum("gxl,cgpl->gcxp", patch, pick, precision=lax.Precision.HIGHEST)
+
+
+def block_geometry(vertices, panel_vertices, block_ids, lattice_cols):
+    corners = block_corners(vertices, panel_vertices, block_ids, lattice_cols)
     centre = (corners[:, 0] + corners[:, 1] + corners[:, 2]) / 3.0
     first_edge = corners[:, 1] - corners[:, 0]
     second_edge = corners[:, 2] - corners[:, 0]
@@ -100,9 +125,10 @@
     high_blocks = segment[1]
     targets = jnp.concatenate([own_blocks, low_blocks])
     sources = jnp.concatenate([own_blocks, high_blocks])
+    lattice_cols = columns * QUAD_COLS + 1
     tiles = tile_block(
-        block_geometry(vertices, panel_vertices, targets),
-        block_geometry(vertices, panel_vertices, sources),
+        block_geometry(vertices, panel_vertices, targets, lattice_cols),
+        block_geometry(vertices, panel_vertices, sources, lattice_cols),
     )
     self_tiles = tiles[:band_rows]
     pair_tiles = tiles[band_rows:]

time: 582 us -> 517 us (0.89)
  local copies, waits for them, and re-layouts: 195 us -> 117 us
  matrix products: 26.2 us -> 33.2 us
    gather x6 -> x122, local copies, waits for them, and re-layouts: 136 us -> 83.1 us  [the longest x4 135 us: block_geometry(): corners = jnp.transpose(vertices[:, panels], (2, 1, 0, 3))]
    unnamed x13 -> x18, local copies, waits for them, and re-layouts: 16.3 us -> 0.12 us
    transpose x2 -> x0, local copies, waits for them, and re-layouts: 11.3 us -> none  [block_geometry(): corners = jnp.transpose(vertices[:, panels], (2, 1, 0, 3))]
    dot_general x0 -> x2, matrix products: none -> 6.98 us  [block_corners(): jnp.einsum('gxl,cgpl->gcxp', patch, pick, precision=lax.Precision.HIGHEST)]
  transfers between devices with their start and end apart: 8 -> 8, of which waited for: 6 -> 6; matrix products, arithmetic and copies ran while one was open for 46% -> 39% of each run, Pallas kernels for 0% -> 0%
where the time goes in v2:
time: 517 us; the launch traced here: 512 us
  waiting for transfers between devices  222 us (43%)
  local copies, waits for them, and re-layouts  117 us (23%)
  other arithmetic  114 us (22%)
  matrix products  33.2 us (6%)
  between operations  14.6 us (3%)
  starting transfers between devices  12 us (2%)
    reduce_scatter x2, waiting for transfers between devices, near_product(): lax.psum_scatter(partial_value, 'col', scatter_dimension=1, tiled=True)  166 us
    gather x120, local copies, waits for them, and re-layouts  81.9 us
    reduce_sum x2, other arithmetic, tile_block(): jnp.sum(distance * distance, axis=1) + 0.01  68.1 us
    all_gather x2, waiting for transfers between devices, near_product(): lax.all_gather(jnp.concatenate([block_values, later], axis=0), 'col', axi...  45.5 us
    div x1, other arithmetic, tile_block(): kernel_sum * target_area[:, :, None] * source_area[:, None, :]  29.2 us
    dot_general x4, matrix products, apply_tiles(): jnp.einsum('grq,gpq->grp', source_values, tile_stack, precision=lax.Preci...  16.4 us
    ppermute x4, starting transfers between devices, shifted(): return lax.ppermute(value, axis, pairs)  11.1 us
    scatter-add x4, other arithmetic, near_product(): partial_value.at[low_row, low_pos].add(to_low).at[high_row, high_pos]  10.5 us
  transfers between devices with their start and end apart: 8, of which 6 were waited for; matrix products, arithmetic and copies ran while one was open for 39% of the time, Pallas kernels for 0%

profile of v2, /device:TPU:8, one launch (start us, length us, event | category | flops | bytes accessed | tf_op | source)
XLA Modules:
  0.0 512.5 jit_solution(15881192994583727060)
XLA Ops:
  17.9 40.4 %while.3 = (s32[]{:T(128)}, f32[3,129,513]{2,1,0:T(8,128)S(1)}, s32[20,3]{0,1:T(4,128)S(1)}, f32[20,3,9,17]{3,2,1,0:T(8,128)S(1)}, s32[]{:T(128)}) while((s32[]{:T(128)}, f32[3,129,513]{2,1,0:T(8,128)S(1)}, s32[20,3]{0,1:T(4,128)S(1)}, f32[20,3,9,17]{3,2,1,0:T(8,128)S(1)}, s32[]{:T(128)}) %tuple.86), condition=%wide.while_cond.1, body=%wide.while_body.1.sunk | while | flops 2 | bytes 49269 | solution.py:53
  58.5 41.9 %while.2 = (s32[]{:T(128)}, f32[3,129,513]{2,1,0:T(8,128)S(1)}, s32[20,3]{0,1:T(4,128)S(1)}, f32[20,3,9,17]{3,2,1,0:T(8,128)S(1)}, s32[]{:T(128)}) while((s32[]{:T(128)}, f32[3,129,513]{2,1,0:T(8,128)S(1)}, s32[20,3]{0,1:T(4,128)S(1)}, f32[20,3,9,17]{3,2,1,0:T(8,128)S(1)}, s32[]{:T(128)}) %tuple.100), condition=%wide.while_cond, body=%wide.while_body.sunk | while | flops 2 | bytes 49269 | solution.py:53
  100.6 3.5 fusion.28
  104.7 3.5 fusion.29
  113.7 34.2 %multiply_reduce_fusion.15 = (f32[20,256,256]{2,1,0:T(8,128)}, f32[20,256,256]{2,1,0:T(8,128)}, f32[20,256,256]{2,1,0:T(8,128)}, f32[20,256,256]{2,1,0:T(8,128)}...) fusion(f32[20,3,256]{2,1,0:T(4,128)S(1)} %copy.117, ...), kind=kLoop, calls=%fused_computation.31 | loop fusion | flops 83886080 | bytes 42496000 | tf_op jit(solution)/shard_map/reduce_sum | solution.py:93
  147.9 33.9 %multiply_reduce_fusion.14 = (f32[20,256,256]{2,1,0:T(8,128)}, f32[20,256,256]{2,1,0:T(8,128)}, f32[20,256,256]{2,1,0:T(8,128)}, f32[20,256,256]{2,1,0:T(8,128)}...) fusion(f32[20,3,256]{2,1,0:T(4,128)S(1)} %get-tuple-element.94, ...), kind=kLoop, calls=%fused_computation.30 | loop fusion | flops 83886080 | bytes 42496000 | tf_op jit(solution)/shard_map/reduce_sum | solution.py:95
  181.8 29.2 %fusion.18 = f32[20,256,256]{2,1,0:T(8,128)} fusion(f32[20,256,256]{2,1,0:T(8,128)} %get-tuple-element.41, f32[20,256,256]{2,1,0:T(8,128)} %get-tuple-element.33, f32[20,256,256]{2,1,0:T(8,128)} %get-tuple-element.40, f32[20,256,256]{2,1,0:T(8,128)} %get-tuple-element.32, f32[20,256,256]{2,1,0:T(8,128)} %get-tuple-element.39, ...), kind=kLoop, calls=%fused_computation.53 | loop fusion | flops 64225280 | bytes 89169920 | tf_op jit(solution)/shard_map/div | solution.py:96
  211.1 2.8 gather_fusion.2
  213.9 5.7 %fusion.26 = f32[16,16,256]{2,1,0:T(8,128)S(1)} fusion(f32[16,16,256]{2,1,0:T(8,128)S(1)} %gather_fusion.2, f32[20,256,256]{2,1,0:T(8,128)} %fusion.18), kind=kOutput, calls=%fused_computation.61 | convolution fusion | flops 201326592 | bytes 4718592 | tf_op jit(solution)/shard_map/grq,gpq->grp/dot_general | solution.py:100
  219.6 2.8 gather_fusion.5
  222.4 4.3 fusion.24
  226.7 2.6 broadcast.572.clone
  229.3 2.7 scatter_fusion
  231.9 2.6 scatter_fusion.1
  234.5 4.8 copy.149
  239.4 84.7 %reduce-scatter.3.cloned.1.call-done = f32[8,1,16,256]{3,2,0,1:T(8,128)} async-done(((f32[8,32,16,256]{3,2,0,1:T(8,128)}), f32[8,1,16,256]{3,2,0,1:T(8,128)}) %reduce-scatter.3.cloned.1.call-update) | async-done | bytes 131088 | tf_op jit(solution)/shard_map/reduce_scatter | solution.py:156
  324.9 3.4 collective-permute-start.1
  328.3 2.7 collective-permute-done.1
  335.2 4.2 collective-permute-done.2
  340.4 45.5 %all-gather.5.cloned.1.call-done = f32[8,32,16,256]{3,2,0,1:T(8,128)} async-done(((f32[8,1,16,256]{3,2,0,1:T(8,128)}), f32[8,32,16,256]{3,2,0,1:T(8,128)}) %all-gather.5.cloned.1.call-update) | async-done | bytes 4194320 | tf_op jit(solution)/shard_map/all_gather | solution.py:149
  385.9 2.8 gather_fusion.7
  388.7 4.3 fusion.20
  393.0 2.8 gather_fusion.6
  395.8 5.7 %fusion.22 = f32[16,16,256]{2,1,0:T(8,128)S(1)} fusion(f32[16,16,256]{2,1,0:T(8,128)S(1)} %gather_fusion.6, f32[20,256,256]{2,1,0:T(8,128)} %fusion.18), kind=kOutput, calls=%fused_computation.57 | convolution fusion | flops 201326592 | bytes 4718592 | tf_op jit(solution)/shard_map/grq,gpq->grp/dot_general | solution.py:100
  401.5 2.6 broadcast.572
  404.1 2.7 scatter_fusion.2
  406.7 2.6 scatter_fusion.3
  409.3 4.8 copy.150
  414.2 81.7 %reduce-scatter.5.cloned.1.call-done = f32[8,1,16,256]{3,2,0,1:T(8,128)} async-done(((f32[8,32,16,256]{3,2,0,1:T(8,128)}), f32[8,1,16,256]{3,2,0,1:T(8,128)}) %reduce-scatter.5.cloned.1.call-update) | async-done | bytes 131088 | tf_op jit(solution)/shard_map/reduce_scatter | solution.py:156
  496.8 3.4 collective-permute-start.3
  500.1 2.8 collective-permute-done.3
  502.9 2.8 fusion.47
  (226 shorter events, 105.5 us)
Async XLA Ops:
  7.2 5.3 %copy-start = (s32[3,131072]{1,0:T(4,128)S(1)}, s32[3,131072]{1,0:T(4,128)}, u32[]{:S(2)}) copy-start(s32[3,131072]{1,0:T(4,128)} %param.10) | copy-start | bytes 4718596
  7.2 203.9 %all-gather.3.cloned.1.call-start = ((), (), s32[]{:S(2)}) async-start(), calls=%async_computation.2 | async-start | bytes 4325376 | tf_op jit(solution)/shard_map/all_gather | solution.py:149
  7.2 105.2 %collective-permute-start = (f32[4,1,16,256]{3,2,1,0:T(8,128)}, f32[4,1,16,256]{3,2,1,0:T(8,128)S(1)}, u32[]{:S(2)}, u32[]{:S(2)}) collective-permute-start(f32[4,1,16,256]{3,2,1,0:T(8,128)} %param.7), channel_id=1, source_target_pairs={{32,0},{64,32},{96,64},{33,1},{65,33},{97,65},{34,2},{66,34},{98,6... | collective-permute-start | bytes 196616 | tf_op jit(solution)/shard_map/ppermute | solution.py:18
  15.4 88.7 %copy-start.5 = (f32[8,3,1,1]{0,1,3,2:T(4,128)S(1)}, f32[8,3,1,1]{0,1,3,2:T(4,128)}, u32[]{:S(2)}) copy-start(f32[8,3,1,1]{0,1,3,2:T(4,128)} %constant.268) | copy-start | bytes 292
  104.1 4.9 copy-start.6
  108.2 4.2 copy-start.4
  113.1 210.9 %reduce-scatter.3.cloned.1.call-start = ((), (), s32[]{:S(2)}) async-start(), calls=%async_computation.3 | async-start | bytes 4325376 | tf_op jit(solution)/shard_map/reduce_scatter | solution.py:156
  147.9 33.9 %copy-start.2 = (f32[20,256,256]{2,1,0:T(8,128)S(1)}, f32[20,256,256]{2,1,0:T(8,128)}, u32[]{:S(2)}) copy-start(f32[20,256,256]{2,1,0:T(8,128)} %get-tuple-element.26) | copy-start | bytes 15728644
  239.4 146.6 %all-gather.5.cloned.1.call-start = ((), (), s32[]{:S(2)}) async-start(), calls=%async_computation.4 | async-start | bytes 4325376 | tf_op jit(solution)/shard_map/all_gather | solution.py:149
  324.9 6.1 %collective-permute-start.1 = (f32[4,1,16,256]{3,2,0,1:T(8,128)S(1)}, f32[4,1,16,256]{3,2,0,1:T(8,128)S(1)}, u32[]{:S(2)}, u32[]{:S(2)}) collective-permute-start(f32[4,1,16,256]{3,2,0,1:T(8,128)S(1)} %slice.278), channel_id=1, source_target_pairs={{0,32},{32,64},{64,96},{1,33},{33,65},{65,97},{2,34},{34,66},{66,9... | collective-permute-start | bytes 196616 | tf_op jit(solution)/shard_map/ppermute | solution.py:18
  333.3 169.6 %copy-start.3 = (f32[4,1,16,256]{3,2,0,1:T(8,128)}, f32[4,1,16,256]{3,2,0,1:T(8,128)S(1)}, u32[]{:S(2)}) copy-start(f32[4,1,16,256]{3,2,0,1:T(8,128)S(1)} %fusion.48) | copy-start | bytes 196612
  333.3 6.2 %collective-permute-start.2 = (f32[4,1,16,256]{3,2,0,1:T(8,128)S(1)}, f32[4,1,16,256]{3,2,0,1:T(8,128)S(1)}, u32[]{:S(2)}, u32[]{:S(2)}) collective-permute-start(f32[4,1,16,256]{3,2,0,1:T(8,128)S(1)} %fusion.48), channel_id=1, source_target_pairs={{32,0},{64,32},{96,64},{33,1},{65,33},{97,65},{34,2},{66,34},{98,6... | collective-permute-start | bytes 196616 | tf_op jit(solution)/shard_map/ppermute | solution.py:18
  340.1 155.8 %reduce-scatter.5.cloned.1.call-start = ((), (), s32[]{:S(2)}) async-start(), calls=%async_computation.5 | async-start | bytes 4325376 | tf_op jit(solution)/shard_map/reduce_scatter | solution.py:156
  406.7 99.0 %copy-start.1 = (s32[3,131072]{1,0:T(4,128)S(1)}, s32[3,131072]{1,0:T(4,128)}, u32[]{:S(2)}) copy-start(s32[3,131072]{1,0:T(4,128)} %param.10) | copy-start | bytes 4718596
  496.8 6.1 %collective-permute-start.3 = (f32[4,1,16,256]{3,2,0,1:T(8,128)S(1)}, f32[4,1,16,256]{3,2,0,1:T(8,128)S(1)}, u32[]{:S(2)}, u32[]{:S(2)}) collective-permute-start(f32[4,1,16,256]{3,2,0,1:T(8,128)S(1)} %slice.280), channel_id=1, source_target_pairs={{0,32},{32,64},{64,96},{1,33},{33,65},{65,97},{2,34},{34,66},{66,9... | collective-permute-start | bytes 196616 | tf_op jit(solution)/shard_map/ppermute | solution.py:18
Sparse Core Ops, SparseCore 0:
  113.3 48.8 all-gather.2
  239.5 84.5 reduce-scatter.2
  340.3 45.6 all-gather.4
  414.3 81.5 reduce-scatter.4
